TPU v7x, 512 devices: a whole 4x8x8 slice. The times are simulated.
512 devices in a mesh: row: 16 (over z_hi, x, core), col: 32 (over y, z_lo).
Axes of the slice: x: 4, y: 8, z: 8 (z_hi: 2, z_lo: 4; z = z_hi * 4 + z_lo), core: 2. Of those that a mesh axis runs over, the one named last changes fastest.
Arguments:
- trunk: bfloat16 [4096, 512], P('row', 'col'), may hold values from -6 to 6
- proj_weight: bfloat16 [512, 128], P('col'), may hold values from -0.25 to 0.25
- conv_kernel: bfloat16 [9, 64, 64], replicated, may hold values from -0.25 to 0.25
- norm_gain: float32 [64], replicated, may hold values from 0.1 to 1.9
- norm_bias: float32 [64], replicated, may hold values from -3 to 3
Outputs:
- contact_map: bfloat16 [4096, 64, 4096], P('row', None, 'col')
All inputs are finite; a program needn't handle non-finite values.
Results may differ from a plain program's by a relative error of at most 0.0095.
Values may be sent and summed in bfloat16 or wider, within the bound.
No kernel may reach another device: no remote copies, remote signals or barrier semaphores. Data moves between devices by JAX's collectives and lax.ppermute only.
A program may use at most 128 MiB of HBM per device.

v0:
```python
import jax
import jax.numpy as jnp
from jax import lax
from jax.sharding import PartitionSpec as P

CONV_DILATION = 4


def pair_features(rows, cols, width):
    row_u = rows[:, :width].astype(jnp.float32)
    row_v = rows[:, width:].astype(jnp.float32)
    col_u = cols[:, :width].astype(jnp.float32).T
    col_v = cols[:, width:].astype(jnp.float32).T
    pair_block = row_u[:, :, None] * col_u[None] + row_v[:, :, None] + col_v[None]
    return pair_block.astype(jnp.bfloat16)


def inside_mask(first_entry, count_total, total_bins):
    position_index = (
        first_entry - CONV_DILATION + jnp.arange(count_total + 2 * CONV_DILATION, dtype=jnp.int32)
    )
    return ((position_index >= 0) & (position_index < total_bins)).astype(jnp.bfloat16)


def symmetric_conv(active, conv_kernel):
    width = conv_kernel.shape[1]
    grid = conv_kernel.reshape(3, 3, width, width).transpose(2, 3, 0, 1)
    stacked = jnp.concatenate([grid, grid.transpose(0, 1, 3, 2)], 0)
    result = lax.conv_general_dilated(
        active[None],
        stacked,
        (1, 1),
        "VALID",
        rhs_dilation=(CONV_DILATION, CONV_DILATION),
        dimension_numbers=("NHCW", "OIHW", "NHCW"),
        preferred_element_type=jnp.float32,
    )[0]
    return 0.5 * (result[:, :width] + result[:, width:])


def per_device(trunk, proj_weight, conv_kernel, norm_gain, norm_bias):
    block_rows = trunk.shape[0]
    width = norm_gain.shape[0]
    total_bins = block_rows * lax.axis_size("row")
    block_columns = total_bins // lax.axis_size("col")
    row_begin = lax.axis_index("row") * block_rows
    column_begin = lax.axis_index("col") * block_columns
    partial_sum = jnp.dot(trunk, proj_weight, preferred_element_type=jnp.float32)
    summed = lax.psum(partial_sum, "col").astype(jnp.bfloat16)
    feature_rows = lax.all_gather(summed, "row", axis=0, tiled=True)
    padded_map = jnp.pad(feature_rows, ((CONV_DILATION, CONV_DILATION), (0, 0)))
    widened_rows = lax.dynamic_slice_in_dim(
        padded_map, row_begin, block_rows + 2 * CONV_DILATION, 0
    )
    widened_columns = lax.dynamic_slice_in_dim(
        padded_map, column_begin, block_columns + 2 * CONV_DILATION, 0
    )
    row_keep = inside_mask(row_begin, block_rows, total_bins)
    col_keep = inside_mask(column_begin, block_columns, total_bins)
    widened_pair = (
        pair_features(widened_rows, widened_columns, width)
        * row_keep[:, None, None]
        * col_keep[None, None, :]
    )
    active = jnp.maximum(widened_pair, jnp.zeros((), jnp.bfloat16))
    base_offset = widened_pair[
        CONV_DILATION : CONV_DILATION + block_rows, :, CONV_DILATION : CONV_DILATION + block_columns
    ]
    half_sum = symmetric_conv(active, conv_kernel)
    result = (
        base_offset.astype(jnp.float32)
        + norm_gain[None, :, None] * half_sum
        + norm_bias[None, :, None]
    )
    return result.astype(jnp.bfloat16)


def solution(mesh):
    in_specs = (P("row", "col"), P("col", None), P(), P(), P())
    out_specs = P("row", None, "col")
    return jax.shard_map(
        per_device, mesh=mesh, in_specs=in_specs, out_specs=out_specs, check_vma=False
    )
```

profile of v0, /device:TPU:6, one launch (start us, length us, event | category | flops | bytes accessed | tf_op | source)
XLA Modules:
  0.0 329.9 jit_solution(3806741830517226296)
XLA Ops:
  6.5 0.0 copy-start
  6.5 0.0 all-gather.2.cloned.1.call-start
  6.5 0.7 copy-done
  7.2 0.9 fusion.32
  8.1 156.6 %all-reduce.2 = bf16[256,128]{1,0:T(8,128)(2,1)} all-reduce(f32[256,128]{1,0:T(8,128)S(1)} %fusion.32), channel_id=1, replica_groups=mesh['row'=16,'col'=32] {'col'}, use_global_device_ids=true, to_apply=%region_0.0 | all-reduce | flops 32768 | bytes 196608 | tf_op jit(solution)/shard_map/psum | solution.py:49
  164.7 0.0 all-gather.2.cloned.1.call-update
  164.7 1.0 copy.16
  165.8 1.1 copy.15
  166.8 0.1 slice.34
  166.9 0.1 slice.35
  167.0 0.7 broadcast_multiply_fusion
  167.7 57.4 %all-gather.2.cloned.1.call-done = bf16[4096,128]{1,0:T(8,128)(2,1)} async-done(((bf16[256,128]{1,0:T(8,128)(2,1)}), bf16[4096,128]{1,0:T(8,128)(2,1)}) %all-gather.2.cloned.1.call-update) | async-done | bytes 1048592 | tf_op jit(solution)/shard_map/all_gather | solution.py:50
  225.0 1.1 fusion.23
  226.1 0.1 copy.11
  226.2 0.1 copy.12
  226.3 0.9 convert_bitcast_fusion.1
  227.3 5.7 %fusion.19 = bf16[1,264,64,136]{1,2,3,0:T(8,128)(2,1)} fusion(f32[64,136]{0,1:T(8,128)S(1)} %get-tuple-element.8, f32[264,64]{0,1:T(8,128)S(1)} %copy.12, f32[64,136]{0,1:T(8,128)S(1)} %get-tuple-element.7, f32[264,64]{0,1:T(8,128)S(1)} %copy.11, bf16[136]{0:T(256)(128)(2,1)S(1)} %and_convert_fusion, bf16[264]{0:T(512)(128)(2,1)S(1)} %fusion.28), kind=kLoop, calls=%fused_computation.22 | loop fusion | flops 16084992 | bytes 4801312 | tf_op jit(solution)/shard_map/max | solution.py:65
  233.1 0.0 copy-start.3
  233.1 22.0 %copy.14 = bf16[264,64,1,8,17]{1,3,4,0,2:T(8,128)(2,1)} copy(bf16[264,64,1,8,17]{0,1,4,3,2:T(8,128)(2,1)} %bitcast.21) | data formatting | bytes 9191424 | tf_op jit(solution)/shard_map/conv_general_dilated | solution.py:29
  255.1 5.6 %slice.36 = bf16[264,64,1,7,8]{1,3,4,0,2:T(8,128)(2,1)} slice(bf16[264,64,1,8,17]{1,3,4,0,2:T(8,128)(2,1)} %copy.14), slice={[0:264], [0:64], [0:1], [1:8], [0:8]} | slice | bytes 3784704 | tf_op jit(solution)/shard_map/conv_general_dilated | solution.py:29
  260.7 0.0 copy-done.3
  260.7 19.8 %broadcast_select_fusion = f32[256,8,17,128]{3,1,2,0:T(8,128)} fusion(pred[8,17]{0,1:T(8,128)(4,1)S(1)} %copy-done.3, bf16[264,64,1,7,8]{1,3,4,0,2:T(8,128)(2,1)} %slice.36, bf16[264,64,1,8,17]{1,3,4,0,2:T(8,128)(2,1)} %copy.14, bf16[64,64,3,3]{0,1,3,2:T(8,128)(2,1)S(1)} %bitcast.24, bf16[64,64,3,3]{0,1,3,2:T(8,128)(2,1)S(1)} %bitcast.25), kind=kOutput, calls=%fused_computation.16 | convolution fusion | flops 5158854656 | bytes 24461448 | tf_op jit(solution)/shard_map/conv_general_dilated | solution.py:29
  280.5 14.9 %copy.17 = f32[256,8,17,128]{3,0,2,1:T(8,128)} copy(f32[256,8,17,128]{3,1,2,0:T(8,128)} %broadcast_select_fusion) | data formatting | bytes 35651584 | tf_op jit(solution)/shard_map/conv_general_dilated | solution.py:29
  295.4 0.0 copy-start.2
  295.4 6.9 %slice_bitcast_fusion = f32[256,128,128]{1,0,2:T(8,128)S(1)} fusion(f32[256,1,136,128]{3,0,2,1:T(8,128)} %bitcast.20), kind=kLoop, calls=%fused_computation.7 | loop fusion | bytes 33554432 | tf_op jit(solution)/shard_map/squeeze | solution.py:29
  302.3 0.0 copy-done.2
  302.3 0.0 copy-start.1
  302.3 9.2 %fusion.4 = bf16[256,64,128]{1,0,2:T(8,128)(2,1)} fusion(f32[256,128,128]{1,0,2:T(8,128)S(1)} %slice_bitcast_fusion, f32[64,128]{0,1:T(8,128)S(1)} %slice.33, f32[256,64]{1,0:T(8,128)S(1)} %slice.32, f32[64,128]{0,1:T(8,128)S(1)} %slice.31, f32[256,64]{1,0:T(8,128)S(1)} %slice.30, f32[64]{0:T(128)S(1)} %copy-done.2, f32[64]{0:T(128)S(1)} %broadcast_multiply_fusion, ...), kind=kLoop, calls=%fused_computation.6 | loop fusion | flops 25165824 | bytes 21169408 | tf_op jit(solution)/shard_map/convert_element_type | solution.py:75
  311.6 11.5 %copy.18 = bf16[256,64,128]{2,1,0:T(8,128)(2,1)} copy(bf16[256,64,128]{1,0,2:T(8,128)(2,1)} %fusion.4) | data formatting | bytes 8388608 | tf_op jit(solution)/shard_map/convert_element_type | solution.py:75
  323.1 0.0 copy-done.1
  (6 shorter events, 0.1 us)
Async XLA Ops:
  6.5 0.7 copy-start
  6.5 218.5 %all-gather.2.cloned.1.call-start = ((), (), s32[]{:S(2)}) async-start(), calls=%async_computation | async-start | bytes 1114112 | tf_op jit(solution)/shard_map/all_gather | solution.py:50
  233.1 27.7 %copy-start.3 = (pred[8,17]{0,1:T(8,128)(4,1)S(1)}, pred[8,17]{0,1:T(8,128)(4,1)}, u32[]{:S(2)}) copy-start(pred[8,17]{0,1:T(8,128)(4,1)} %constant.38) | copy-start | bytes 412
  295.4 6.9 %copy-start.2 = (f32[64]{0:T(128)S(1)}, f32[64]{0:T(128)}, u32[]{:S(2)}) copy-start(f32[64]{0:T(128)} %param.9) | copy-start | bytes 772
  302.3 20.8 %copy-start.1 = (bf16[256,16]{0,1:T(8,128)(2,1)S(1)}, bf16[256,16]{0,1:T(8,128)(2,1)}, u32[]{:S(2)}) copy-start(bf16[256,16]{0,1:T(8,128)(2,1)} %param.5) | copy-start | bytes 24580
Sparse Core Ops, SparseCore 0:
  164.8 60.1 all-gather.1
where the time goes:
time: 332 us; the launch traced here: 330 us
  blocking collectives  157 us (47%)
  local copies, waits for them, and re-layouts  64.2 us (19%)
  waiting for transfers between devices  57.4 us (17%)
  matrix products  20.6 us (6%)
  other arithmetic  17.7 us (5%)
  between operations  13.5 us (4%)
    psum x1, blocking collectives, per_device(): summed = lax.psum(partial_sum, 'col').astype(jnp.bfloat16)  157 us
    all_gather x1, waiting for transfers between devices, per_device(): feature_rows = lax.all_gather(summed, 'row', axis=0, tiled=True)  57.4 us
    conv_general_dilated x3, local copies, waits for them, and re-layouts, symmetric_conv(): lax.conv_general_dilated(active[None], stacked, (1, 1), 'VALID', rhs_dila...  42.5 us
    conv_general_dilated x1, matrix products, symmetric_conv(): lax.conv_general_dilated(active[None], stacked, (1, 1), 'VALID', rhs_dila...  19.8 us
    convert_element_type x1, local copies, waits for them, and re-layouts, per_device(): return result.astype(jnp.bfloat16)  11.5 us
    convert_element_type x1, other arithmetic, per_device(): return result.astype(jnp.bfloat16)  9.23 us
    squeeze x1, local copies, waits for them, and re-layouts, symmetric_conv(): lax.conv_general_dilated(active[None], stacked, (1, 1), 'VALID', rhs_dila...  6.93 us
  transfers between devices with their start and end apart: 1, of which 1 were waited for; matrix products, arithmetic and copies ran while one was open for 1% of the time, Pallas kernels for 0%

commit v1 on v0

v1 whole, which is shorter than its diff:
```python
import jax
import jax.numpy as jnp
from jax import lax
from jax.experimental import pallas as pl
from jax.experimental.pallas import tpu as pltpu
from jax.sharding import PartitionSpec as P

DIL = 4
CH = 64
FAR = -1e30
GROUP = 4
STEP_ROWS = GROUP * DIL
LANES = 128
TAPS_IN = GROUP + 2
VMEM_BYTES = 48 << 20


def pack_kernel(trunk_ref, proj_ref, send_ref):
    row = lax.axis_index("row")
    n_col, channels = send_ref.shape[0], send_ref.shape[1]
    rows = trunk_ref.shape[2]
    last = trunk_ref.shape[0] - 1
    above = trunk_ref[jnp.maximum(row - 1, 0), :, rows - LANES :].astype(jnp.float32)
    below = trunk_ref[jnp.minimum(row + 1, last), :, :LANES].astype(jnp.float32)
    lane = lax.broadcasted_iota(jnp.int32, (channels, LANES), 1)
    row_sides = jnp.where(lane < LANES // 2, pltpu.roll(below, 8, 1), pltpu.roll(above, LANES - 8, 1))
    row_sides = row_sides.astype(jnp.bfloat16)
    own = trunk_ref[row]
    proj = proj_ref[...]

    def chunk(c):
        c = min(max(c, 0), n_col - 1)
        return trunk_ref[c // 2, :, (c % 2) * LANES : (c % 2 + 1) * LANES]

    for c in range(n_col):
        sides = jnp.where(lane < 8, chunk(c + 1), row_sides)
        sides = jnp.where(lane >= LANES - 8, chunk(c - 1), sides)
        send_ref[c] = jnp.concatenate([own, chunk(c), sides, proj], 1)


def weights_kernel(kernel_ref, gain_ref, weights_ref):
    weights_ref[...] = jnp.zeros_like(weights_ref)
    half_gain = 0.5 * gain_ref[...]
    for b in range(3):
        for a in range(3):
            total = kernel_ref[3 * a + b].astype(jnp.float32) + kernel_ref[3 * b + a].astype(jnp.float32)
            tap = (half_gain * total).astype(jnp.bfloat16)
            for out in range(GROUP):
                first = (b * TAPS_IN + out + a) * CH
                weights_ref[out * CH : (out + 1) * CH, first : first + CH] = tap


def map_kernel(
    gathered_ref, weights_ref, bias_ref, out_ref,
    rows_ref, cols_ref, act_ref, pair_ref, bias_tile,
    *, rows,
):
    step = pl.program_id(0)
    row, col = lax.axis_index("row"), lax.axis_index("col")
    n_row, n_col = lax.axis_size("row"), lax.axis_size("col")

    def generate(row_index_block, slot_of):
        block, count = row_index_block
        for local in range(count):
            q, s = local // DIL, local % DIL
            u = jnp.broadcast_to(block[:CH, local : local + 1], (CH, LANES))
            v = jnp.broadcast_to(block[CH:, local : local + 1], (CH, LANES))
            lanes = slice((s % 2) * LANES, (s % 2 + 1) * LANES)
            for b in range(3):
                pair = (u * cols_ref[b, :CH] + (v + cols_ref[b, CH:])).astype(jnp.bfloat16)
                if b == 1:
                    pair_ref[s // 2, slot_of(q), :, lanes] = pair
                act_ref[b, s // 2, slot_of(q), :, lanes] = jnp.maximum(pair, jnp.zeros((), jnp.bfloat16))

    @pl.when(step == 0)
    def _():
        got = gathered_ref[...]
        bins = rows + 2 * LANES
        feat = lax.dot_general(
            got[:, :bins], got[:, bins:], (((0,), (0,)), ((), ())), preferred_element_type=jnp.float32
        ).astype(jnp.bfloat16).astype(jnp.float32)
        far = jnp.where(lax.broadcasted_iota(jnp.int32, (8, 2 * CH), 1) >= CH, FAR, 0.0)
        sides = feat[rows + LANES :]
        rows_ref[0:8] = jnp.where(row == 0, far, sides[LANES - 16 : LANES - 8])
        rows_ref[8 : 8 + rows] = feat[:rows]
        rows_ref[8 + rows : 16 + rows] = jnp.where(row == n_row - 1, far, sides[8:16])
        rows_ref[16 + rows :] = jnp.zeros((LANES, 2 * CH), jnp.float32)
        left = jnp.where(col == 0, far, sides[LANES - 8 :])
        right = jnp.where(col == n_col - 1, far, sides[:8])
        rest = jnp.zeros((LANES - 16, 2 * CH), jnp.float32)
        window = jnp.concatenate([left, feat[rows : rows + LANES], right, rest], 0)
        turned = window.T
        for b in range(3):
            first = 8 + (b - 1) * DIL
            cols_ref[b] = turned[:, first : first + LANES]
        bias_tile[...] = jnp.broadcast_to(bias_ref[...], (CH, LANES))
        start = rows_ref[0:LANES].T
        generate((start[:, 4:12], 8), lambda q: q)
        generate((start[:, 12:28], 16), lambda q: q + 2)

    for half in range(2):
        taken = [
            act_ref[b, half, pl.ds(GROUP * step, TAPS_IN)].reshape(TAPS_IN * CH, 2 * LANES) for b in range(3)
        ]
        result = jnp.dot(weights_ref[...], jnp.concatenate(taken, 0), preferred_element_type=jnp.float32)
        for out in range(GROUP):
            for h in range(2):
                lanes = slice(h * LANES, (h + 1) * LANES)
                base = pair_ref[half, GROUP * step + 1 + out, :, lanes].astype(jnp.float32)
                value = base + result[out * CH : (out + 1) * CH, lanes] + bias_tile[...]
                out_ref[DIL * out + 2 * half + h] = value.astype(out_ref.dtype)

    nxt = jnp.minimum(step + 1, rows // STEP_ROWS - 1)
    block = rows_ref[pl.ds(pl.multiple_of(STEP_ROWS * nxt + 8, 8), LANES)].T
    generate((block[:, 4:20], 16), lambda q: GROUP * nxt + 2 + q)


def local_map(gathered, conv_kernel, norm_gain, norm_bias):
    rows = gathered.shape[1] - 3 * LANES
    depth = 3 * TAPS_IN * CH
    weights = pl.pallas_call(
        weights_kernel,
        out_shape=jax.ShapeDtypeStruct((GROUP * CH, depth), jnp.bfloat16),
        name="weights",
    )(conv_kernel, norm_gain[:, None])

    whole = lambda shape: pl.BlockSpec(shape, lambda i: (0,) * len(shape))
    n_q = rows // DIL
    return pl.pallas_call(
        lambda *refs: map_kernel(*refs, rows=rows),
        grid=(rows // STEP_ROWS,),
        in_specs=[
            whole(gathered.shape), whole((GROUP * CH, depth)), whole((CH, 1)),
        ],
        out_specs=pl.BlockSpec((STEP_ROWS, CH, LANES), lambda i: (i, 0, 0)),
        out_shape=jax.ShapeDtypeStruct((rows, CH, LANES), jnp.bfloat16),
        scratch_shapes=[
            pltpu.VMEM((rows + 16 + LANES, 2 * CH), jnp.float32),
            pltpu.VMEM((3, 2 * CH, LANES), jnp.float32),
            pltpu.VMEM((3, 2, n_q + 2, CH, 2 * LANES), jnp.bfloat16),
            pltpu.VMEM((2, n_q + 2, CH, 2 * LANES), jnp.bfloat16),
            pltpu.VMEM((CH, LANES), jnp.float32),
        ],
        compiler_params=pltpu.CompilerParams(
            dimension_semantics=("arbitrary",), vmem_limit_bytes=VMEM_BYTES
        ),
        name="pair_map",
    )(gathered, weights, norm_bias[:, None])


def per_device(trunk, proj_weight, conv_kernel, norm_gain, norm_bias):
    rows, channels = trunk.shape
    n_row, n_col = lax.axis_size("row"), lax.axis_size("col")

    every_bin = lax.all_to_all(
        jnp.broadcast_to(trunk.T[None], (n_row, channels, rows)), "row", 0, 0, tiled=True
    )
    width = rows + 3 * LANES
    send = pl.pallas_call(
        pack_kernel,
        out_shape=jax.ShapeDtypeStruct((n_col, channels, width), jnp.bfloat16),
        name="pack",
    )(every_bin, proj_weight)
    gathered = lax.all_to_all(send, "col", 0, 0, tiled=True).reshape(n_col * channels, width)
    return local_map(gathered, conv_kernel, norm_gain, norm_bias)


def solution(mesh):
    in_specs = (P("row", "col"), P("col", None), P(), P(), P())
    out_specs = P("row", None, "col")
    return jax.shard_map(
        per_device, mesh=mesh, in_specs=in_specs, out_specs=out_specs, check_vma=False
    )
```

time: 332 us -> 71.8 us (0.22)
  blocking collectives: 157 us -> 21.8 us
  local copies, waits for them, and re-layouts: 64.2 us -> 3.87 us
  waiting for transfers between devices: 57.4 us -> 17.1 us
  matrix products: 20.6 us -> 0 us
  other arithmetic: 17.7 us -> 0 us
  Pallas kernels: 0 us -> 16.8 us
  between operations: 13.5 us -> 0.02 us
  starting transfers between devices: 0.01 us -> 10.9 us
    psum x1 -> x0, blocking collectives: 157 us -> none  [per_device(): summed = lax.psum(partial_sum, 'col').astype(jnp.bfloat16)]
    all_gather x1 -> x0, waiting for transfers between devices: 57.4 us -> none  [per_device(): feature_rows = lax.all_gather(summed, 'row', axis=0, tiled=True)]
    conv_general_dilated x3 -> x0, local copies, waits for them, and re-layouts: 42.5 us -> none  [symmetric_conv(): lax.conv_general_dilated(active[None], stacked, (1, 1), 'VALID', rhs_dila...]
    all_to_all x0 -> x1, blocking collectives: none -> 21.8 us  [per_device(): lax.all_to_all(jnp.broadcast_to(trunk.T[None], (n_row, channels, rows)),...]
    conv_general_dilated x1 -> x0, matrix products: 19.8 us -> none  [symmetric_conv(): lax.conv_general_dilated(active[None], stacked, (1, 1), 'VALID', rhs_dila...]
    all_to_all x0 -> x1, waiting for transfers between devices: none -> 17.1 us  [per_device(): lax.all_to_all(send, 'col', 0, 0, tiled=True)]
    pallas_call x0 -> x3, Pallas kernels: none -> 16.8 us  [the longest x1 13 us: local_map(): pl.pallas_call(lambda *refs: map_kernel(*refs, rows=rows), grid=(rows //...]
    convert_element_type x3 -> x0, local copies, waits for them, and re-layouts: 11.8 us -> none  [the longest x1 11.5 us: per_device(): return result.astype(jnp.bfloat16)]
  transfers between devices with their start and end apart: 1 -> 1, of which waited for: 1 -> 1; matrix products, arithmetic and copies ran while one was open for 1% -> 3% of each run, Pallas kernels for 0% -> 3%
where the time goes in v1:
time: 71.8 us; the launch traced here: 70.4 us
  blocking collectives  21.8 us (30%)
  waiting for transfers between devices  17.1 us (24%)
  Pallas kernels  16.8 us (23%)
  starting transfers between devices  10.9 us (15%)
  local copies, waits for them, and re-layouts  3.87 us (5%)
    all_to_all x1, blocking collectives, per_device(): lax.all_to_all(jnp.broadcast_to(trunk.T[None], (n_row, channels, rows)),...  21.8 us
    all_to_all x1, waiting for transfers between devices, per_device(): lax.all_to_all(send, 'col', 0, 0, tiled=True)  17.1 us
    pallas_call x1, Pallas kernels, local_map(): pl.pallas_call(lambda *refs: map_kernel(*refs, rows=rows), grid=(rows //...  13 us
    all_to_all x1, starting transfers between devices, per_device(): lax.all_to_all(send, 'col', 0, 0, tiled=True)  10.9 us
    pallas_call x1, Pallas kernels, local_map(): pl.pallas_call(weights_kernel, out_shape=jax.ShapeDtypeStruct((GROUP * CH...  1.94 us
    pallas_call x1, Pallas kernels, per_device(): pl.pallas_call(pack_kernel, out_shape=jax.ShapeDtypeStruct((n_col, channe...  1.86 us
  transfers between devices with their start and end apart: 1, of which 1 were waited for; matrix products, arithmetic and copies ran while one was open for 3% of the time, Pallas kernels for 3%

profile of v1, /device:TPU:6, one launch (start us, length us, event | category | flops | bytes accessed | tf_op | source)
XLA Modules:
  0.0 70.4 jit_solution(15891937259093841454)
XLA Ops:
  0.0 0.7 %broadcast_in_dim.12 = bf16[16,16,256]{2,1,0:T(8,128)(2,1)S(1)} broadcast(bf16[16,256]{1,0:T(8,128)(2,1)} %bitcast.5), dimensions={1,2} | broadcast | bytes 139264 | tf_op jit(solution)/shard_map/broadcast_in_dim | solution.py:156
  0.7 21.8 %all_to_all.10.trunk_ref = bf16[16,16,256]{2,1,0:T(8,128)(2,1)} all-to-all(bf16[16,16,256]{2,1,0:T(8,128)(2,1)S(1)} %broadcast_in_dim.12), channel_id=1, replica_groups=mesh['row'=16,'col'=32] {'row'}, dimensions={0} | all-to-all | bytes 262144 | tf_op jit(solution)/shard_map/all_to_all | solution.py:155
  22.5 1.9 %pack.1 = bf16[32,16,640]{2,1,0:T(8,128)(2,1)} custom-call(bf16[16,16,256]{2,1,0:T(8,128)(2,1)} %all_to_all.10.trunk_ref, bf16[16,128]{1,0:T(8,128)(2,1)} %proj_ref.1), custom_call_target="tpu_custom_call" | custom-call | tf_op jit(solution)/shard_map/pack/pallas_call | solution.py:159
  24.3 10.9 %all-to-all-start.1 = ((bf16[32,16,640]{2,1,0:T(8,128)(2,1)}), bf16[32,16,640]{2,1,0:T(8,128)(2,1)S(1)}, u32[]{:S(2)}, u32[]{:S(2)}) async-start(bf16[32,16,640]{2,1,0:T(8,128)(2,1)} %pack.1), calls=%async_computation.1 | async-start | bytes 1310720 | tf_op jit(solution)/shard_map/all_to_all | solution.py:164
  35.2 1.4 %copy.6.gain_ref = f32[64,1]{1,0:T(8,128)} copy(f32[64,1]{0,1:T(1,128)} %bitcast.6) | data formatting | bytes 512 | tf_op jit(solution)/shard_map/broadcast_in_dim | solution.py:125
  36.6 0.7 %copy.7.refs_2_ = f32[64,1]{1,0:T(8,128)S(1)} copy(f32[64,1]{0,1:T(1,128)} %bitcast.7) | data formatting | bytes 512 | tf_op jit(solution)/shard_map/broadcast_in_dim | solution.py:148
  37.3 1.9 %weights.1.refs_1_ = bf16[256,1152]{1,0:T(8,128)(2,1)} custom-call(bf16[9,64,64]{2,1,0:T(8,128)(2,1)} %kernel_ref.1, f32[64,1]{1,0:T(8,128)} %copy.6.gain_ref), custom_call_target="tpu_custom_call" | custom-call | tf_op jit(solution)/shard_map/weights/pallas_call | solution.py:121
  39.3 17.1 %all-to-all-done.1 = bf16[32,16,640]{2,1,0:T(8,128)(2,1)S(1)} async-done(((bf16[32,16,640]{2,1,0:T(8,128)(2,1)}), bf16[32,16,640]{2,1,0:T(8,128)(2,1)S(1)}, u32[]{:S(2)}, u32[]{:S(2)}) %all-to-all-start.1) | async-done | bytes 655392 | tf_op jit(solution)/shard_map/all_to_all | solution.py:164
  56.3 0.0 copy-start
  56.3 1.1 %copy-done = bf16[256,1152]{1,0:T(8,128)(2,1)S(1)} copy-done((bf16[256,1152]{1,0:T(8,128)(2,1)S(1)}, bf16[256,1152]{1,0:T(8,128)(2,1)}, u32[]{:S(2)}) %copy-start) | copy-done | bytes 589848
  57.4 13.0 %pair_map.1 = bf16[256,64,128]{2,1,0:T(8,128)(2,1)} custom-call(bf16[512,640]{1,0:T(8,128)(2,1)S(1)} %bitcast.4, bf16[256,1152]{1,0:T(8,128)(2,1)S(1)} %copy-done, f32[64,1]{1,0:T(8,128)S(1)} %copy.7.refs_2_), custom_call_target="tpu_custom_call" | custom-call | tf_op jit(solution)/shard_map/pair_map/pallas_call | solution.py:129
Async XLA Ops:
  24.3 32.0 %all-to-all-start.1 = ((bf16[32,16,640]{2,1,0:T(8,128)(2,1)}), bf16[32,16,640]{2,1,0:T(8,128)(2,1)S(1)}, u32[]{:S(2)}, u32[]{:S(2)}) async-start(bf16[32,16,640]{2,1,0:T(8,128)(2,1)} %pack.1), calls=%async_computation.1 | async-start | bytes 1310720 | tf_op jit(solution)/shard_map/all_to_all | solution.py:164
  56.3 1.1 %copy-start = (bf16[256,1152]{1,0:T(8,128)(2,1)S(1)}, bf16[256,1152]{1,0:T(8,128)(2,1)}, u32[]{:S(2)}) copy-start(bf16[256,1152]{1,0:T(8,128)(2,1)} %weights.1.refs_1_) | copy-start | bytes 1769476

commit v2 on v1

--- a/solution.py
+++ b/solution.py
@@ -15,27 +15,56 @@
 VMEM_BYTES = 48 << 20
 
 
-def pack_kernel(trunk_ref, proj_ref, send_ref):
+def pack_kernel(trunk_ref, above_ref, below_ref, proj_ref, send_ref):
+    channels, rows = trunk_ref.shape
+    part = channels // 2
+    lane = lax.broadcasted_iota(jnp.int32, (channels, LANES), 1)
+    sides = jnp.where(
+        lane < LANES // 2,
+        below_ref[:, :LANES].astype(jnp.float32),
+        above_ref[:, rows - LANES :].astype(jnp.float32),
+    )
+    turned = pltpu.roll(sides[part:], LANES // 2, 1)
+    inner = (lane[:part] >= LANES // 4) & (lane[:part] < LANES - LANES // 4)
+    block = jnp.concatenate(
+        [
+            trunk_ref[:, :LANES], trunk_ref[:, LANES:], proj_ref[...],
+            jnp.where(inner, turned, sides[:part]).astype(jnp.bfloat16),
+        ],
+        0,
+    )
+    for peer in range(send_ref.shape[0]):
+        send_ref[peer] = block
+
+
+def features_kernel(got_ref, rows_ref, window_ref):
+    peers, height, _ = got_ref.shape
+    channels = 2 * height // 7
+    part = channels // 2
+
+    def take(first, count):
+        return got_ref[:, first : first + count].reshape(peers * count, LANES)
+
+    def project(bins, proj):
+        return lax.dot_general(bins, proj, (((0,), (0,)), ((), ())), preferred_element_type=jnp.float32)
+
+    proj = take(2 * channels, channels)
+    sides = take(3 * channels, part)
+    one = project(sides, take(2 * channels, part))
+    two = project(sides, take(2 * channels + part, part))
+    half = LANES // 2
+    below = one[:8] + two[half : half + 8]
+    above = one[LANES - 8 :] + two[half - 8 : half]
     row = lax.axis_index("row")
-    n_col, channels = send_ref.shape[0], send_ref.shape[1]
-    rows = trunk_ref.shape[2]
-    last = trunk_ref.shape[0] - 1
-    above = trunk_ref[jnp.maximum(row - 1, 0), :, rows - LANES :].astype(jnp.float32)
-    below = trunk_ref[jnp.minimum(row + 1, last), :, :LANES].astype(jnp.float32)
-    lane = lax.broadcasted_iota(jnp.int32, (channels, LANES), 1)
-    row_sides = jnp.where(lane < LANES // 2, pltpu.roll(below, 8, 1), pltpu.roll(above, LANES - 8, 1))
-    row_sides = row_sides.astype(jnp.bfloat16)
-    own = trunk_ref[row]
-    proj = proj_ref[...]
-
-    def chunk(c):
-        c = min(max(c, 0), n_col - 1)
-        return trunk_ref[c // 2, :, (c % 2) * LANES : (c % 2 + 1) * LANES]
-
-    for c in range(n_col):
-        sides = jnp.where(lane < 8, chunk(c + 1), row_sides)
-        sides = jnp.where(lane >= LANES - 8, chunk(c - 1), sides)
-        send_ref[c] = jnp.concatenate([own, chunk(c), sides, proj], 1)
+    far = jnp.where(lax.broadcasted_iota(jnp.int32, (8, 2 * CH), 1) >= CH, FAR, 0.0)
+    above = jnp.where(row == 0, far, above)
+    below = jnp.where(row == lax.axis_size("row") - 1, far, below)
+    feat = jnp.concatenate(
+        [above, project(take(0, channels), proj), project(take(channels, channels), proj), below], 0
+    ).astype(jnp.bfloat16)
+    rows_ref[...] = feat
+    height = LANES + 16
+    window_ref[...] = jnp.where(lax.axis_index("col") % 2 == 1, feat[LANES:], feat[:height])
 
 
 def weights_kernel(kernel_ref, gain_ref, weights_ref):
@@ -51,13 +80,11 @@
 
 
 def map_kernel(
-    gathered_ref, weights_ref, bias_ref, out_ref,
+    feat_ref, window_ref, weights_ref, bias_ref, out_ref,
     rows_ref, cols_ref, act_ref, pair_ref, bias_tile,
     *, rows,
 ):
     step = pl.program_id(0)
-    row, col = lax.axis_index("row"), lax.axis_index("col")
-    n_row, n_col = lax.axis_size("row"), lax.axis_size("col")
 
     def generate(row_index_block, slot_of):
         block, count = row_index_block
@@ -74,21 +101,10 @@
 
     @pl.when(step == 0)
     def _():
-        got = gathered_ref[...]
-        bins = rows + 2 * LANES
-        feat = lax.dot_general(
-            got[:, :bins], got[:, bins:], (((0,), (0,)), ((), ())), preferred_element_type=jnp.float32
-        ).astype(jnp.bfloat16).astype(jnp.float32)
-        far = jnp.where(lax.broadcasted_iota(jnp.int32, (8, 2 * CH), 1) >= CH, FAR, 0.0)
-        sides = feat[rows + LANES :]
-        rows_ref[0:8] = jnp.where(row == 0, far, sides[LANES - 16 : LANES - 8])
-        rows_ref[8 : 8 + rows] = feat[:rows]
-        rows_ref[8 + rows : 16 + rows] = jnp.where(row == n_row - 1, far, sides[8:16])
+        rows_ref[: 16 + rows] = feat_ref[...].astype(jnp.float32)
         rows_ref[16 + rows :] = jnp.zeros((LANES, 2 * CH), jnp.float32)
-        left = jnp.where(col == 0, far, sides[LANES - 8 :])
-        right = jnp.where(col == n_col - 1, far, sides[:8])
         rest = jnp.zeros((LANES - 16, 2 * CH), jnp.float32)
-        window = jnp.concatenate([left, feat[rows : rows + LANES], right, rest], 0)
+        window = jnp.concatenate([window_ref[...].astype(jnp.float32), rest], 0)
         turned = window.T
         for b in range(3):
             first = 8 + (b - 1) * DIL
@@ -115,12 +131,12 @@
     generate((block[:, 4:20], 16), lambda q: GROUP * nxt + 2 + q)
 
 
-def local_map(gathered, conv_kernel, norm_gain, norm_bias):
-    rows = gathered.shape[1] - 3 * LANES
+def local_map(feat, window, conv_kernel, norm_gain, norm_bias):
+    rows = feat.shape[0] - 16
     depth = 3 * TAPS_IN * CH
     weights = pl.pallas_call(
         weights_kernel,
-        out_shape=jax.ShapeDtypeStruct((GROUP * CH, depth), jnp.bfloat16),
+        out_shape=pltpu.VMEM((GROUP * CH, depth), jnp.bfloat16),
         name="weights",
     )(conv_kernel, norm_gain[:, None])
 
@@ -130,7 +146,7 @@
         lambda *refs: map_kernel(*refs, rows=rows),
         grid=(rows // STEP_ROWS,),
         in_specs=[
-            whole(gathered.shape), whole((GROUP * CH, depth)), whole((CH, 1)),
+            whole(feat.shape), whole(window.shape), whole((GROUP * CH, depth)), whole((CH, 1)),
         ],
         out_specs=pl.BlockSpec((STEP_ROWS, CH, LANES), lambda i: (i, 0, 0)),
         out_shape=jax.ShapeDtypeStruct((rows, CH, LANES), jnp.bfloat16),
@@ -145,24 +161,56 @@
             dimension_semantics=("arbitrary",), vmem_limit_bytes=VMEM_BYTES
         ),
         name="pair_map",
-    )(gathered, weights, norm_bias[:, None])
+    )(feat, window, weights, norm_bias[:, None])
+
+
+def window_routes(n_row, n_col):
+    targets = [[0, x, core] for x in (0, 1, 3, 2) for core in (0, 1)]
+    targets += [[1, x, core] for x in (0, 1, 3, 2) for core in (0, 1)]
+    routes = []
+    for r in range(n_row):
+        for parity in range(2):
+            sources = list(range(parity, n_col, 2))
+            to_rows = list(range(n_row))
+            if (n_row, n_col) == (16, 32):
+                column_y = (2 * r + parity) // 4
+                away = [min((c // 4 - column_y) % 8, (column_y - c // 4) % 8) for c in range(n_col)]
+                sources.sort(key=lambda c: -away[c])
+                to_rows = [
+                    ((r // 8) ^ zh) * 8 + ((r // 2 % 4 + x) % 4) * 2 + ((r % 2) ^ core)
+                    for zh, x, core in targets
+                ]
+            routes += [(r * n_col + c, t * n_col + 2 * r + parity) for c, t in zip(sources, to_rows)]
+    return routes
+
+
+def in_vmem(array):
+    return pltpu.with_memory_space_constraint(array, pltpu.VMEM)
 
 
 def per_device(trunk, proj_weight, conv_kernel, norm_gain, norm_bias):
     rows, channels = trunk.shape
     n_row, n_col = lax.axis_size("row"), lax.axis_size("col")
 
-    every_bin = lax.all_to_all(
-        jnp.broadcast_to(trunk.T[None], (n_row, channels, rows)), "row", 0, 0, tiled=True
-    )
-    width = rows + 3 * LANES
+    own = trunk.T
+    above = lax.ppermute(own, "row", [(r, r + 1) for r in range(n_row - 1)])
+    below = lax.ppermute(own, "row", [(r + 1, r) for r in range(n_row - 1)])
     send = pl.pallas_call(
         pack_kernel,
-        out_shape=jax.ShapeDtypeStruct((n_col, channels, width), jnp.bfloat16),
+        out_shape=pltpu.VMEM((n_col, 7 * channels // 2, LANES), jnp.bfloat16),
         name="pack",
-    )(every_bin, proj_weight)
-    gathered = lax.all_to_all(send, "col", 0, 0, tiled=True).reshape(n_col * channels, width)
-    return local_map(gathered, conv_kernel, norm_gain, norm_bias)
+    )(own, in_vmem(above), in_vmem(below), proj_weight)
+    got = lax.all_to_all(send, "col", 0, 0, tiled=True)
+    feat, window = pl.pallas_call(
+        features_kernel,
+        out_shape=[
+            pltpu.VMEM((rows + 16, 2 * CH), jnp.bfloat16),
+            pltpu.VMEM((LANES + 16, 2 * CH), jnp.bfloat16),
+        ],
+        name="features",
+    )(in_vmem(got))
+    window = lax.ppermute(window, ("row", "col"), window_routes(n_row, n_col))
+    return local_map(feat, window, conv_kernel, norm_gain, norm_bias)
 
 
 def solution(mesh):

time: 71.8 us -> 65.5 us (0.912)
  the two profiles are of different devices: /device:TPU:6 before, /device:TPU:48 now
where the time goes in v2:
time: 65.5 us; the launch traced here: 65.2 us
  blocking collectives  27.8 us (42%)
  starting transfers between devices  19.6 us (30%)
  Pallas kernels  14.6 us (22%)
  local copies, waits for them, and re-layouts  2.1 us (3%)
  waiting for transfers between devices  1.02 us (2%)
    all_to_all x1, blocking collectives, per_device(): got = lax.all_to_all(send, 'col', 0, 0, tiled=True)  27.8 us
    ppermute x1, starting transfers between devices, per_device(): window = lax.ppermute(window, ('row', 'col'), window_routes(n_row, n_col))  15.3 us
    pallas_call x1, Pallas kernels, local_map(): pl.pallas_call(lambda *refs: map_kernel(*refs, rows=rows), grid=(rows //...  12.4 us
    ppermute x1, starting transfers between devices, per_device(): above = lax.ppermute(own, 'row', [(r, r + 1) for r in range(n_row - 1)])  3.03 us
    broadcast_in_dim x1, local copies, waits for them, and re-layouts, local_map(): norm_gain[:, None]  1.36 us
  transfers between devices with their start and end apart: 3, of which 1 were waited for; matrix products, arithmetic and copies ran while one was open for 3% of the time, Pallas kernels for 2%

profile of v2, /device:TPU:48, one launch (start us, length us, event | category | flops | bytes accessed | tf_op | source)
XLA Modules:
  0.0 65.2 jit_solution(7679799970813990139)
XLA Ops:
  0.0 1.3 %collective-permute-start.1 = (bf16[16,256]{1,0:T(8,128)(2,1)}, bf16[16,256]{1,0:T(8,128)(2,1)S(1)}, u32[]{:S(2)}, u32[]{:S(2)}) collective-permute-start(bf16[16,256]{1,0:T(8,128)(2,1)} %bitcast.3), channel_id=1, source_target_pairs={{32,0},{64,32},{96,64},{128,96},{160,128},{192,160},{224,192},{256... | collective-permute-start | bytes 24584 | tf_op jit(solution)/shard_map/ppermute | solution.py:197
  1.3 3.0 %collective-permute-start = (bf16[16,256]{1,0:T(8,128)(2,1)}, bf16[16,256]{1,0:T(8,128)(2,1)S(1)}, u32[]{:S(2)}, u32[]{:S(2)}) collective-permute-start(bf16[16,256]{1,0:T(8,128)(2,1)} %bitcast.4), channel_id=1, source_target_pairs={{0,32},{32,64},{64,96},{96,128},{128,160},{160,192},{192,224},{224... | collective-permute-start | bytes 24584 | tf_op jit(solution)/shard_map/ppermute | solution.py:196
  4.3 0.0 collective-permute-done.1.below_ref
  4.3 1.0 %collective-permute-done.above_ref = bf16[16,256]{1,0:T(8,128)(2,1)S(1)} collective-permute-done((bf16[16,256]{1,0:T(8,128)(2,1)}, bf16[16,256]{1,0:T(8,128)(2,1)S(1)}, u32[]{:S(2)}, u32[]{:S(2)}) %collective-permute-start) | collective-permute-done | bytes 8224 | tf_op jit(solution)/shard_map/ppermute | solution.py:196
  5.3 0.8 %pack.1 = bf16[32,56,128]{2,1,0:T(8,128)(2,1)S(1)} custom-call(bf16[16,256]{1,0:T(8,128)(2,1)} %bitcast.5, bf16[16,256]{1,0:T(8,128)(2,1)S(1)} %collective-permute-done.above_ref, bf16[16,256]{1,0:T(8,128)(2,1)S(1)} %collective-permute-done.1.below_ref, bf16[16,128]{1,0:T(8,128)(2,1)} %proj_ref.1), custom_call_target="tpu_custom_call" | custom-call | tf_op jit(solution)/shard_map/pack/pallas_call | solution.py:198
  6.1 27.8 %all_to_all.5.got_ref = bf16[32,56,128]{2,1,0:T(8,128)(2,1)S(1)} all-to-all(bf16[32,56,128]{2,1,0:T(8,128)(2,1)S(1)} %pack.1), channel_id=1, replica_groups=mesh['row'=16,'col'=32] {'col'}, dimensions={0} | all-to-all | bytes 917504 | tf_op jit(solution)/shard_map/all_to_all | solution.py:203
  33.9 0.3 features.1
  34.2 15.3 %collective-permute-start.2 = (bf16[144,128]{1,0:T(8,128)(2,1)S(1)}, bf16[144,128]{1,0:T(8,128)(2,1)S(1)}, u32[]{:S(2)}, u32[]{:S(2)}) collective-permute-start(bf16[144,128]{1,0:T(8,128)(2,1)S(1)} %get-tuple-element.8), channel_id=1, source_target_pairs={{16,0},{18,32},{12,64},{14,96},{20,192},{22,224},{8,128},{10,160},... | collective-permute-start | bytes 110600 | tf_op jit(solution)/shard_map/ppermute | solution.py:212
  49.6 1.4 %copy.6.gain_ref = f32[64,1]{1,0:T(8,128)} copy(f32[64,1]{0,1:T(1,128)} %bitcast.6) | data formatting | bytes 512 | tf_op jit(solution)/shard_map/broadcast_in_dim | solution.py:141
  50.9 0.7 %copy.7.refs_3_ = f32[64,1]{1,0:T(8,128)S(1)} copy(f32[64,1]{0,1:T(1,128)} %bitcast.7) | data formatting | bytes 512 | tf_op jit(solution)/shard_map/broadcast_in_dim | solution.py:164
  51.7 1.1 %weights.1.refs_2_ = bf16[256,1152]{1,0:T(8,128)(2,1)S(1)} custom-call(bf16[9,64,64]{2,1,0:T(8,128)(2,1)} %kernel_ref.1, f32[64,1]{1,0:T(8,128)} %copy.6.gain_ref), custom_call_target="tpu_custom_call" | custom-call | tf_op jit(solution)/shard_map/weights/pallas_call | solution.py:137
  52.8 0.0 collective-permute-done.2.refs_1_
  52.8 12.4 %pair_map.1 = bf16[256,64,128]{2,1,0:T(8,128)(2,1)} custom-call(bf16[272,128]{1,0:T(8,128)(2,1)S(1)} %get-tuple-element.7.refs_0_, bf16[144,128]{1,0:T(8,128)(2,1)S(1)} %collective-permute-done.2.refs_1_, bf16[256,1152]{1,0:T(8,128)(2,1)S(1)} %weights.1.refs_2_, f32[64,1]{1,0:T(8,128)S(1)} %copy.7.refs_3_), custom_call_target="tpu_custom_call" | custom-call | tf_op jit(solution)/shard_map/pair_map/pallas_call | solution.py:145
Async XLA Ops:
  0.0 4.3 %collective-permute-start.1 = (bf16[16,256]{1,0:T(8,128)(2,1)}, bf16[16,256]{1,0:T(8,128)(2,1)S(1)}, u32[]{:S(2)}, u32[]{:S(2)}) collective-permute-start(bf16[16,256]{1,0:T(8,128)(2,1)} %bitcast.3), channel_id=1, source_target_pairs={{32,0},{64,32},{96,64},{128,96},{160,128},{192,160},{224,192},{256... | collective-permute-start | bytes 24584 | tf_op jit(solution)/shard_map/ppermute | solution.py:197
  1.3 4.1 %collective-permute-start = (bf16[16,256]{1,0:T(8,128)(2,1)}, bf16[16,256]{1,0:T(8,128)(2,1)S(1)}, u32[]{:S(2)}, u32[]{:S(2)}) collective-permute-start(bf16[16,256]{1,0:T(8,128)(2,1)} %bitcast.4), channel_id=1, source_target_pairs={{0,32},{32,64},{64,96},{96,128},{128,160},{160,192},{192,224},{224... | collective-permute-start | bytes 24584 | tf_op jit(solution)/shard_map/ppermute | solution.py:196
  34.2 18.6 %collective-permute-start.2 = (bf16[144,128]{1,0:T(8,128)(2,1)S(1)}, bf16[144,128]{1,0:T(8,128)(2,1)S(1)}, u32[]{:S(2)}, u32[]{:S(2)}) collective-permute-start(bf16[144,128]{1,0:T(8,128)(2,1)S(1)} %get-tuple-element.8), channel_id=1, source_target_pairs={{16,0},{18,32},{12,64},{14,96},{20,192},{22,224},{8,128},{10,160},... | collective-permute-start | bytes 110600 | tf_op jit(solution)/shard_map/ppermute | solution.py:212

commit v3 on v2

v3 whole, which is shorter than its diff:
```python
import jax
import jax.numpy as jnp
from jax import lax
from jax.experimental import pallas as pl
from jax.experimental.pallas import tpu as pltpu
from jax.sharding import PartitionSpec as P

DIL = 4
CH = 64
FAR = -1e30
GROUP = 4
STEP_ROWS = GROUP * DIL
LANES = 128
TAPS_IN = GROUP + 2
RING = 4
PIECE = 8
OUT_ORDER = (1, 2, 3, 0)
VMEM_BYTES = 48 << 20


def pack_kernel(trunk_ref, one_ref, two_ref, proj_ref, send_ref):
    channels, rows = trunk_ref.shape
    part = channels // 2
    lane = lax.broadcasted_iota(jnp.int32, (channels, LANES), 1)
    one_is_above = lax.axis_index("row") % 2 == 1

    def side(lanes, from_one):
        return jnp.where(from_one, one_ref[:, lanes], two_ref[:, lanes]).astype(jnp.float32)

    below = side(slice(0, LANES), ~one_is_above)
    above = side(slice(rows - LANES, rows), one_is_above)
    sides = jnp.where(lane < LANES // 2, below, above)
    turned = pltpu.roll(sides[part:], LANES // 2, 1)
    inner = (lane[:part] >= LANES // 4) & (lane[:part] < LANES - LANES // 4)
    block = jnp.concatenate(
        [
            trunk_ref[:, :LANES], trunk_ref[:, LANES:], proj_ref[...],
            jnp.where(inner, turned, sides[:part]).astype(jnp.bfloat16),
        ],
        0,
    )
    for peer in range(send_ref.shape[0]):
        send_ref[peer] = block


def features_kernel(got_ref, rows_ref, window_ref):
    peers, height, _ = got_ref.shape
    channels = 2 * height // 7
    part = channels // 2

    def take(first, count):
        return got_ref[:, first : first + count].reshape(peers * count, LANES)

    def project(bins, proj):
        return lax.dot_general(bins, proj, (((0,), (0,)), ((), ())), preferred_element_type=jnp.float32)

    proj = take(2 * channels, channels)
    sides = take(3 * channels, part)
    one = project(sides, take(2 * channels, part))
    two = project(sides, take(2 * channels + part, part))
    half = LANES // 2
    below = one[:8] + two[half : half + 8]
    above = one[LANES - 8 :] + two[half - 8 : half]
    row = lax.axis_index("row")
    far = jnp.where(lax.broadcasted_iota(jnp.int32, (8, 2 * CH), 1) >= CH, FAR, 0.0)
    above = jnp.where(row == 0, far, above)
    below = jnp.where(row == lax.axis_size("row") - 1, far, below)
    feat = jnp.concatenate(
        [above, project(take(0, channels), proj), project(take(channels, channels), proj), below], 0
    ).astype(jnp.bfloat16)
    rows_ref[...] = feat
    height = LANES + 16
    window_ref[...] = jnp.where(serves_odd(row, lax.axis_index("col")), feat[LANES:], feat[:height])


def weights_kernel(kernel_ref, gain_ref, bias_ref, weights_ref, twice_ref):
    twice_ref[...] = jnp.concatenate([bias_ref[...]] * 2, 1)
    weights_ref[...] = jnp.zeros_like(weights_ref)
    half_gain = 0.5 * gain_ref[...]
    for b in range(3):
        for a in range(3):
            total = kernel_ref[3 * a + b].astype(jnp.float32) + kernel_ref[3 * b + a].astype(jnp.float32)
            tap = (half_gain * total.T).astype(jnp.bfloat16)
            for place, out in enumerate(OUT_ORDER):
                first = (b * TAPS_IN + out + a) * CH
                weights_ref[first : first + CH, place * CH : (place + 1) * CH] = tap


def map_kernel(feat_ref, window_ref, weights_ref, bias_ref, out_ref, shift_ref, row_u, row_v, cols_ref, *rest, rows):
    acts, pairs, (stage_ref, sems) = rest[:RING], rest[RING : 2 * RING], rest[2 * RING :]
    step = pl.program_id(0)

    def positive(pair):
        return jnp.maximum(pair, jnp.zeros((), jnp.bfloat16))

    def generate(u_rows, v_rows, first, ring, place):
        for s in range(DIL):
            u = jnp.broadcast_to(u_rows[first + s : first + s + 1], (LANES, LANES))
            v = jnp.broadcast_to(v_rows[first + s : first + s + 1], (LANES, LANES))
            for b in range(3):
                pair = (u * cols_ref[b, 0] + (v + cols_ref[b, 1])).astype(jnp.bfloat16)
                if b == 1:
                    pairs[ring][place, s] = pair
                else:
                    acts[ring][b // 2, place, s] = positive(pair)

    def copies(group):
        return [
            pltpu.make_async_copy(
                stage_ref.at[pl.ds(STEP_ROWS * group + first, PIECE)],
                out_ref.at[pl.ds(STEP_ROWS * group + first, PIECE)],
                sems.at[group, first // PIECE],
            )
            for first in range(0, STEP_ROWS, PIECE)
        ]

    @pl.when(step == 0)
    def _():
        low = lax.broadcasted_iota(jnp.int32, (rows + 16, LANES), 1) < CH
        here = feat_ref[...].astype(jnp.float32)
        shift_ref[: rows + 16] = here
        ahead = shift_ref[DIL : DIL + rows + 16]
        row_u[: rows + 16] = jnp.where(low, here, pltpu.roll(ahead, CH, 1))
        row_v[: rows + 16] = jnp.where(low, pltpu.roll(here, CH, 1), ahead)
        window = window_ref[...].astype(jnp.float32)
        turned = pltpu.roll(window, CH, 1)
        height = LANES + 16
        for part, (left, right) in enumerate(((window, turned), (turned, window))):
            shift_ref[:height] = jnp.where(low[:height], left, right)
            for b in range(3):
                cols_ref[b, part] = shift_ref[4 + DIL * b : 4 + DIL * b + LANES]
        for chunk in range(3):
            base = 8 * chunk
            ring, place = ((RING - 1, 1), (0, 0), (0, 1))[chunk]
            generate(row_u[base : base + 8], row_v[base : base + 8], DIL, ring, place)

    low = lax.broadcasted_iota(jnp.int32, (LANES, LANES), 1) < CH
    bias = bias_ref[...]

    for which in range(RING):
        group = RING * step + which
        old = (which - 1) % RING
        first = pl.multiple_of(STEP_ROWS * group + 24, 8)
        u_rows = row_u[pl.ds(first, 16)]
        v_rows = row_v[pl.ds(first, 16)]
        for place in range(2):
            generate(u_rows, v_rows, 8 * place + DIL, (which + 1) % RING, place)
        taken = []
        for b in range(3):
            for ring, place in ((old, 1), (which, 0), (which, 1)):
                rows_in = positive(pairs[ring][place]) if b == 1 else acts[ring][b // 2, place]
                taken.append(rows_in.reshape(DIL * LANES, LANES))
        result = jnp.dot(jnp.concatenate(taken, 1), weights_ref[...], preferred_element_type=jnp.float32)
        for s in range(DIL):
            here = slice(s * LANES, (s + 1) * LANES)
            mixed = jnp.where(low, pairs[which][1, s].astype(jnp.float32), pairs[old][1, s].astype(jnp.float32))
            bases = (pairs[which][0, s].astype(jnp.float32), mixed)
            for side, base in enumerate(bases):
                value = base + result[here, side * LANES : (side + 1) * LANES] + bias
                flat = value.astype(out_ref.dtype).T
                for e in range(2):
                    row = STEP_ROWS * group + DIL * OUT_ORDER[2 * side + e] + s
                    stage_ref[row] = flat[e * CH : (e + 1) * CH]
        for copy in copies(group):
            copy.start()

    @pl.when(step == rows // (RING * STEP_ROWS) - 1)
    def _():
        for group in range(rows // STEP_ROWS):
            for copy in copies(group):
                copy.wait()


def local_map(feat, window, conv_kernel, norm_gain, norm_bias):
    rows = feat.shape[0] - 16
    depth = 3 * TAPS_IN * CH
    weights, bias = pl.pallas_call(
        weights_kernel,
        out_shape=[
            pltpu.VMEM((depth, GROUP * CH), jnp.bfloat16),
            pltpu.VMEM((1, 2 * CH), jnp.float32),
        ],
        name="weights",
    )(conv_kernel, norm_gain[None], norm_bias[None])

    whole = lambda shape: pl.BlockSpec(shape, lambda i: (0,) * len(shape))
    act = pltpu.VMEM((2, 2, DIL, LANES, LANES), jnp.bfloat16)
    pair = pltpu.VMEM((2, DIL, LANES, LANES), jnp.bfloat16)
    features = pltpu.VMEM((rows + 48, LANES), jnp.float32)
    return pl.pallas_call(
        lambda *refs: map_kernel(*refs, rows=rows),
        grid=(rows // (RING * STEP_ROWS),),
        in_specs=[whole(feat.shape), whole(window.shape), whole((depth, GROUP * CH)), whole((1, 2 * CH))],
        out_specs=pl.BlockSpec(memory_space=pl.ANY),
        out_shape=jax.ShapeDtypeStruct((rows, CH, LANES), jnp.bfloat16),
        scratch_shapes=[
            features, features, features, pltpu.VMEM((3, 2, LANES, LANES), jnp.float32),
            *[act] * RING, *[pair] * RING,
            pltpu.VMEM((rows, CH, LANES), jnp.bfloat16),
            pltpu.SemaphoreType.DMA((rows // STEP_ROWS, STEP_ROWS // PIECE)),
        ],
        compiler_params=pltpu.CompilerParams(
            dimension_semantics=("arbitrary",), vmem_limit_bytes=VMEM_BYTES
        ),
        name="pair_map",
    )(feat, window, weights, bias)


def hops(source, target):
    total = 0
    for size, place in (
        (4, lambda r, c: r // 2 % 4), (8, lambda r, c: c // 4), (8, lambda r, c: r // 8 * 4 + c % 4),
    ):
        apart = (place(*source) - place(*target)) % size
        total += min(apart, size - apart)
    return total


def pairing(sources, targets):
    for limit in range(16):
        owner = {}

        def settle(source, seen):
            for target in sorted(targets, key=lambda t: hops(source, t)):
                if target in seen or hops(source, target) > limit:
                    continue
                seen.add(target)
                if target not in owner or settle(owner[target], seen):
                    owner[target] = source
                    return True
            return False

        if all(settle(source, set()) for source in sources):
            return {source: target for target, source in owner.items()}
    raise ValueError("no pairing")


def serves_odd(row, col):
    inner = (col % 4 == 1) | (col % 4 == 2)
    return inner ^ (row % 2 == 1)


def window_routes(n_row, n_col):
    routes = []
    for r in range(n_row):
        for odd in range(2):
            sources = [(r, c) for c in range(n_col) if serves_odd(r, c) == odd]
            targets = [(t, 2 * r + odd) for t in range(n_row)]
            for (sr, sc), (tr, tc) in pairing(sources, targets).items():
                routes.append((sr * n_col + sc, tr * n_col + tc))
    return sorted(routes)


def in_vmem(array):
    return pltpu.with_memory_space_constraint(array, pltpu.VMEM)


def per_device(trunk, proj_weight, conv_kernel, norm_gain, norm_bias):
    rows, channels = trunk.shape
    n_row, n_col = lax.axis_size("row"), lax.axis_size("col")

    own = trunk.T
    one = lax.ppermute(own, "row", [(r, r ^ 1) for r in range(n_row)])
    two = lax.ppermute(own, "row", [(r, ((r + 1) ^ 1) - 1) for r in range(1, n_row - 1)])
    send = pl.pallas_call(
        pack_kernel,
        out_shape=pltpu.VMEM((n_col, 7 * channels // 2, LANES), jnp.bfloat16),
        name="pack",
    )(own, in_vmem(one), in_vmem(two), proj_weight)
    got = lax.all_to_all(send, "col", 0, 0, tiled=True)
    feat, window = pl.pallas_call(
        features_kernel,
        out_shape=[
            pltpu.VMEM((rows + 16, 2 * CH), jnp.bfloat16),
            pltpu.VMEM((LANES + 16, 2 * CH), jnp.bfloat16),
        ],
        name="features",
    )(in_vmem(got))
    window = lax.ppermute(window, ("row", "col"), window_routes(n_row, n_col))
    return local_map(feat, window, conv_kernel, norm_gain, norm_bias)


def solution(mesh):
    in_specs = (P("row", "col"), P("col", None), P(), P(), P())
    out_specs = P("row", None, "col")
    return jax.shard_map(
        per_device, mesh=mesh, in_specs=in_specs, out_specs=out_specs, check_vma=False
    )
```

time: 65.5 us -> 62.3 us (0.951)
  the two profiles are of different devices: /device:TPU:48 before, /device:TPU:6 now
where the time goes in v3:
time: 62.3 us; the launch traced here: 62 us
  blocking collectives  27.7 us (44%)
  starting transfers between devices  14.8 us (24%)
  Pallas kernels  11.8 us (19%)
  waiting for transfers between devices  7.67 us (12%)
    all_to_all x1, blocking collectives, per_device(): got = lax.all_to_all(send, 'col', 0, 0, tiled=True)  27.7 us
    ppermute x1, starting transfers between devices, per_device(): one = lax.ppermute(own, 'row', [(r, r ^ 1) for r in range(n_row)])  10.7 us
    pallas_call x1, Pallas kernels, local_map(): pl.pallas_call(lambda *refs: map_kernel(*refs, rows=rows), grid=(rows //...  9.57 us
    ppermute x1, waiting for transfers between devices, per_device(): window = lax.ppermute(window, ('row', 'col'), window_routes(n_row, n_col))  6.66 us
    ppermute x1, starting transfers between devices, per_device(): lax.ppermute(own, 'row', [(r, (r + 1 ^ 1) - 1) for r in range(1, n_row -...  2.16 us
    ppermute x1, starting transfers between devices, per_device(): window = lax.ppermute(window, ('row', 'col'), window_routes(n_row, n_col))  1.92 us
  transfers between devices with their start and end apart: 3, of which 2 were waited for; matrix products, arithmetic and copies ran while one was open for 0% of the time, Pallas kernels for 2%

profile of v3, /device:TPU:6, one launch (start us, length us, event | category | flops | bytes accessed | tf_op | source)
XLA Modules:
  0.0 62.0 jit_solution(4619502732460143571)
XLA Ops:
  0.0 2.2 %collective-permute-start.1 = (bf16[16,256]{1,0:T(8,128)(2,1)}, bf16[16,256]{1,0:T(8,128)(2,1)S(1)}, u32[]{:S(2)}, u32[]{:S(2)}) collective-permute-start(bf16[16,256]{1,0:T(8,128)(2,1)} %bitcast.3), channel_id=1, source_target_pairs={{32,64},{64,32},{96,128},{128,96},{160,192},{192,160},{224,256},{2... | collective-permute-start | bytes 24584 | tf_op jit(solution)/shard_map/ppermute | solution.py:264
  2.2 10.7 %collective-permute-start = (bf16[16,256]{1,0:T(8,128)(2,1)}, bf16[16,256]{1,0:T(8,128)(2,1)S(1)}, u32[]{:S(2)}, u32[]{:S(2)}) collective-permute-start(bf16[16,256]{1,0:T(8,128)(2,1)} %bitcast.4), channel_id=1, source_target_pairs={{0,32},{32,0},{64,96},{96,64},{128,160},{160,128},{192,224},{224,1... | collective-permute-start | bytes 24584 | tf_op jit(solution)/shard_map/ppermute | solution.py:263
  12.9 0.0 collective-permute-done.1.two_ref
  12.9 1.0 %collective-permute-done.one_ref = bf16[16,256]{1,0:T(8,128)(2,1)S(1)} collective-permute-done((bf16[16,256]{1,0:T(8,128)(2,1)}, bf16[16,256]{1,0:T(8,128)(2,1)S(1)}, u32[]{:S(2)}, u32[]{:S(2)}) %collective-permute-start) | collective-permute-done | bytes 8224 | tf_op jit(solution)/shard_map/ppermute | solution.py:263
  13.9 0.8 %pack.1 = bf16[32,56,128]{2,1,0:T(8,128)(2,1)S(1)} custom-call(bf16[16,256]{1,0:T(8,128)(2,1)} %bitcast.5, bf16[16,256]{1,0:T(8,128)(2,1)S(1)} %collective-permute-done.one_ref, bf16[16,256]{1,0:T(8,128)(2,1)S(1)} %collective-permute-done.1.two_ref, bf16[16,128]{1,0:T(8,128)(2,1)} %proj_ref.1), custom_call_target="tpu_custom_call" | custom-call | tf_op jit(solution)/shard_map/pack/pallas_call | solution.py:265
  14.7 27.7 %all_to_all.5.got_ref = bf16[32,56,128]{2,1,0:T(8,128)(2,1)S(1)} all-to-all(bf16[32,56,128]{2,1,0:T(8,128)(2,1)S(1)} %pack.1), channel_id=1, replica_groups=mesh['row'=16,'col'=32] {'col'}, dimensions={0} | all-to-all | bytes 917504 | tf_op jit(solution)/shard_map/all_to_all | solution.py:270
  42.4 0.3 features.1
  42.7 1.9 %collective-permute-start.2 = (bf16[144,128]{1,0:T(8,128)(2,1)S(1)}, bf16[144,128]{1,0:T(8,128)(2,1)S(1)}, u32[]{:S(2)}, u32[]{:S(2)}) collective-permute-start(bf16[144,128]{1,0:T(8,128)(2,1)S(1)} %get-tuple-element.10), channel_id=1, source_target_pairs={{0,160},{1,417},{2,385},{3,320},{4,128},{5,481},{6,449},{7,416},{8... | collective-permute-start | bytes 110600 | tf_op jit(solution)/shard_map/ppermute | solution.py:279
  44.6 1.2 %weights.1 = (bf16[1152,256]{1,0:T(8,128)(2,1)S(1)}, f32[1,128]{1,0:T(1,128)S(1)}) custom-call(bf16[9,64,64]{2,1,0:T(8,128)(2,1)} %kernel_ref.1, f32[1,64]{1,0:T(1,128)} %bitcast.6, f32[1,64]{1,0:T(1,128)} %bitcast.7), custom_call_target="tpu_custom_call" | custom-call | tf_op jit(solution)/shard_map/weights/pallas_call | solution.py:177
  45.8 6.7 %collective-permute-done.2.refs_1_ = bf16[144,128]{1,0:T(8,128)(2,1)S(1)} collective-permute-done((bf16[144,128]{1,0:T(8,128)(2,1)S(1)}, bf16[144,128]{1,0:T(8,128)(2,1)S(1)}, u32[]{:S(2)}, u32[]{:S(2)}) %collective-permute-start.2) | collective-permute-done | bytes 36896 | tf_op jit(solution)/shard_map/ppermute | solution.py:279
  52.5 9.6 %pair_map.1 = bf16[256,64,128]{2,1,0:T(8,128)(2,1)} custom-call(bf16[272,128]{1,0:T(8,128)(2,1)S(1)} %get-tuple-element.9.refs_0_, bf16[144,128]{1,0:T(8,128)(2,1)S(1)} %collective-permute-done.2.refs_1_, bf16[1152,256]{1,0:T(8,128)(2,1)S(1)} %get-tuple-element.11.refs_2_, f32[1,128]{1,0:T(1,128)S(1)} %get-tuple-element.12.refs_3_), custom_call_target="tpu_custom_call" | custom-call | tf_op jit(solution)/shard_map/pair_map/pallas_call | solution.py:190
Async XLA Ops:
  0.0 12.9 %collective-permute-start.1 = (bf16[16,256]{1,0:T(8,128)(2,1)}, bf16[16,256]{1,0:T(8,128)(2,1)S(1)}, u32[]{:S(2)}, u32[]{:S(2)}) collective-permute-start(bf16[16,256]{1,0:T(8,128)(2,1)} %bitcast.3), channel_id=1, source_target_pairs={{32,64},{64,32},{96,128},{128,96},{160,192},{192,160},{224,256},{2... | collective-permute-start | bytes 24584 | tf_op jit(solution)/shard_map/ppermute | solution.py:264
  2.2 11.7 %collective-permute-start = (bf16[16,256]{1,0:T(8,128)(2,1)}, bf16[16,256]{1,0:T(8,128)(2,1)S(1)}, u32[]{:S(2)}, u32[]{:S(2)}) collective-permute-start(bf16[16,256]{1,0:T(8,128)(2,1)} %bitcast.4), channel_id=1, source_target_pairs={{0,32},{32,0},{64,96},{96,64},{128,160},{160,128},{192,224},{224,1... | collective-permute-start | bytes 24584 | tf_op jit(solution)/shard_map/ppermute | solution.py:263
  42.7 9.8 %collective-permute-start.2 = (bf16[144,128]{1,0:T(8,128)(2,1)S(1)}, bf16[144,128]{1,0:T(8,128)(2,1)S(1)}, u32[]{:S(2)}, u32[]{:S(2)}) collective-permute-start(bf16[144,128]{1,0:T(8,128)(2,1)S(1)} %get-tuple-element.10), channel_id=1, source_target_pairs={{0,160},{1,417},{2,385},{3,320},{4,128},{5,481},{6,449},{7,416},{8... | collective-permute-start | bytes 110600 | tf_op jit(solution)/shard_map/ppermute | solution.py:279

commit v4 on v3

--- a/solution.py
+++ b/solution.py
@@ -73,7 +73,19 @@
     window_ref[...] = jnp.where(serves_odd(row, lax.axis_index("col")), feat[LANES:], feat[:height])
 
 
-def weights_kernel(kernel_ref, gain_ref, bias_ref, weights_ref, twice_ref):
+def prepare_kernel(kernel_ref, gain_ref, bias_ref, feat_ref, weights_ref, twice_ref, row_u, row_v, shift_ref):
+    count = feat_ref.shape[0]
+    low = lax.broadcasted_iota(jnp.int32, (count, LANES), 1) < CH
+    here = feat_ref[...].astype(jnp.float32)
+    shift_ref[:count] = here
+    shift_ref[count:] = jnp.zeros_like(shift_ref[count:])
+    ahead = shift_ref[DIL : DIL + count]
+    for ref, value in (
+        (row_u, jnp.where(low, here, pltpu.roll(ahead, CH, 1))),
+        (row_v, jnp.where(low, pltpu.roll(here, CH, 1), ahead)),
+    ):
+        ref[:count] = value
+        ref[count:] = jnp.zeros_like(ref[count:])
     twice_ref[...] = jnp.concatenate([bias_ref[...]] * 2, 1)
     weights_ref[...] = jnp.zeros_like(weights_ref)
     half_gain = 0.5 * gain_ref[...]
@@ -86,7 +98,7 @@
                 weights_ref[first : first + CH, place * CH : (place + 1) * CH] = tap
 
 
-def map_kernel(feat_ref, window_ref, weights_ref, bias_ref, out_ref, shift_ref, row_u, row_v, cols_ref, *rest, rows):
+def map_kernel(row_u, row_v, window_ref, weights_ref, bias_ref, out_ref, shift_ref, cols_ref, short_ref, *rest, rows):
     acts, pairs, (stage_ref, sems) = rest[:RING], rest[RING : 2 * RING], rest[2 * RING :]
     step = pl.program_id(0)
 
@@ -95,14 +107,16 @@
 
     def generate(u_rows, v_rows, first, ring, place):
         for s in range(DIL):
-            u = jnp.broadcast_to(u_rows[first + s : first + s + 1], (LANES, LANES))
-            v = jnp.broadcast_to(v_rows[first + s : first + s + 1], (LANES, LANES))
-            for b in range(3):
-                pair = (u * cols_ref[b, 0] + (v + cols_ref[b, 1])).astype(jnp.bfloat16)
-                if b == 1:
-                    pairs[ring][place, s] = pair
-                else:
-                    acts[ring][b // 2, place, s] = positive(pair)
+            u = jnp.broadcast_to(u_rows[first + s : first + s + 1], (16, LANES))
+            v = jnp.broadcast_to(v_rows[first + s : first + s + 1], (16, LANES))
+            u, v, short_u, short_v = (
+                jnp.broadcast_to(x[None], (LANES // 16, 16, LANES)).reshape(LANES, LANES)
+                for x in (u, v, u.astype(jnp.bfloat16), v.astype(jnp.bfloat16))
+            )
+            pairs[ring][place, s] = (u * cols_ref[1, 0] + (v + cols_ref[1, 1])).astype(jnp.bfloat16)
+            for side in range(2):
+                near = short_u * short_ref[side, 0] + (short_v + short_ref[side, 1])
+                acts[ring][side, place, s] = positive(near)
 
     def copies(group):
         return [
@@ -116,19 +130,15 @@
 
     @pl.when(step == 0)
     def _():
-        low = lax.broadcasted_iota(jnp.int32, (rows + 16, LANES), 1) < CH
-        here = feat_ref[...].astype(jnp.float32)
-        shift_ref[: rows + 16] = here
-        ahead = shift_ref[DIL : DIL + rows + 16]
-        row_u[: rows + 16] = jnp.where(low, here, pltpu.roll(ahead, CH, 1))
-        row_v[: rows + 16] = jnp.where(low, pltpu.roll(here, CH, 1), ahead)
+        low = lax.broadcasted_iota(jnp.int32, (LANES + 16, LANES), 1) < CH
         window = window_ref[...].astype(jnp.float32)
         turned = pltpu.roll(window, CH, 1)
-        height = LANES + 16
         for part, (left, right) in enumerate(((window, turned), (turned, window))):
-            shift_ref[:height] = jnp.where(low[:height], left, right)
+            shift_ref[...] = jnp.where(low, left, right)
             for b in range(3):
                 cols_ref[b, part] = shift_ref[4 + DIL * b : 4 + DIL * b + LANES]
+            for side in range(2):
+                short_ref[side, part] = cols_ref[2 * side, part].astype(jnp.bfloat16)
         for chunk in range(3):
             base = 8 * chunk
             ring, place = ((RING - 1, 1), (0, 0), (0, 1))[chunk]
@@ -174,27 +184,28 @@
 def local_map(feat, window, conv_kernel, norm_gain, norm_bias):
     rows = feat.shape[0] - 16
     depth = 3 * TAPS_IN * CH
-    weights, bias = pl.pallas_call(
-        weights_kernel,
+    row_part = pltpu.VMEM((rows + 48, LANES), jnp.float32)
+    weights, bias, row_u, row_v = pl.pallas_call(
+        prepare_kernel,
         out_shape=[
-            pltpu.VMEM((depth, GROUP * CH), jnp.bfloat16),
-            pltpu.VMEM((1, 2 * CH), jnp.float32),
-        ],
-        name="weights",
-    )(conv_kernel, norm_gain[None], norm_bias[None])
+            pltpu.VMEM((depth, GROUP * CH), jnp.bfloat16), pltpu.VMEM((1, 2 * CH), jnp.float32), row_part, row_part,
+        ],
+        scratch_shapes=[pltpu.VMEM((rows + 32, LANES), jnp.float32)],
+        name="prepare",
+    )(conv_kernel, norm_gain[None], norm_bias[None], feat)
 
     whole = lambda shape: pl.BlockSpec(shape, lambda i: (0,) * len(shape))
     act = pltpu.VMEM((2, 2, DIL, LANES, LANES), jnp.bfloat16)
     pair = pltpu.VMEM((2, DIL, LANES, LANES), jnp.bfloat16)
-    features = pltpu.VMEM((rows + 48, LANES), jnp.float32)
     return pl.pallas_call(
         lambda *refs: map_kernel(*refs, rows=rows),
         grid=(rows // (RING * STEP_ROWS),),
-        in_specs=[whole(feat.shape), whole(window.shape), whole((depth, GROUP * CH)), whole((1, 2 * CH))],
+        in_specs=[whole(a.shape) for a in (row_u, row_v, window, weights, bias)],
         out_specs=pl.BlockSpec(memory_space=pl.ANY),
         out_shape=jax.ShapeDtypeStruct((rows, CH, LANES), jnp.bfloat16),
         scratch_shapes=[
-            features, features, features, pltpu.VMEM((3, 2, LANES, LANES), jnp.float32),
+            pltpu.VMEM((LANES + 16, LANES), jnp.float32), pltpu.VMEM((3, 2, LANES, LANES), jnp.float32),
+            pltpu.VMEM((2, 2, LANES, LANES), jnp.bfloat16),
             *[act] * RING, *[pair] * RING,
             pltpu.VMEM((rows, CH, LANES), jnp.bfloat16),
             pltpu.SemaphoreType.DMA((rows // STEP_ROWS, STEP_ROWS // PIECE)),
@@ -203,7 +214,7 @@
             dimension_semantics=("arbitrary",), vmem_limit_bytes=VMEM_BYTES
         ),
         name="pair_map",
-    )(feat, window, weights, bias)
+    )(row_u, row_v, window, weights, bias)
 
 
 def hops(source, target):

time: 62.3 us -> 62.3 us (level)
  local copies, waits for them, and re-layouts: 0 us -> 0.63 us
    unnamed x0 -> x2, local copies, waits for them, and re-layouts: none -> 0.63 us
where the time goes in v4:
time: 62.3 us; the launch traced here: 62.1 us
  blocking collectives  27.7 us (44%)
  starting transfers between devices  14.8 us (24%)
  Pallas kernels  11.4 us (18%)
  waiting for transfers between devices  7.53 us (12%)
  local copies, waits for them, and re-layouts  0.63 us (1%)
    all_to_all x1, blocking collectives, per_device(): got = lax.all_to_all(send, 'col', 0, 0, tiled=True)  27.7 us
    ppermute x1, starting transfers between devices, per_device(): one = lax.ppermute(own, 'row', [(r, r ^ 1) for r in range(n_row)])  10.7 us
    pallas_call x1, Pallas kernels, local_map(): pl.pallas_call(lambda *refs: map_kernel(*refs, rows=rows), grid=(rows //...  8.98 us
    ppermute x1, waiting for transfers between devices, per_device(): window = lax.ppermute(window, ('row', 'col'), window_routes(n_row, n_col))  6.53 us
    ppermute x1, starting transfers between devices, per_device(): lax.ppermute(own, 'row', [(r, (r + 1 ^ 1) - 1) for r in range(1, n_row -...  2.16 us
    ppermute x1, starting transfers between devices, per_device(): window = lax.ppermute(window, ('row', 'col'), window_routes(n_row, n_col))  1.91 us
    pallas_call x1, Pallas kernels, local_map(): pl.pallas_call(prepare_kernel, out_shape=[pltpu.VMEM((depth, GROUP * CH),...  1.3 us
  transfers between devices with their start and end apart: 3, of which 2 were waited for; matrix products, arithmetic and copies ran while one was open for 0% of the time, Pallas kernels for 2%

profile of v4, /device:TPU:6, one launch (start us, length us, event | category | flops | bytes accessed | tf_op | source)
XLA Modules:
  0.0 62.1 jit_solution(5120466473374778478)
XLA Ops:
  0.0 2.2 %collective-permute-start.1 = (bf16[16,256]{1,0:T(8,128)(2,1)}, bf16[16,256]{1,0:T(8,128)(2,1)S(1)}, u32[]{:S(2)}, u32[]{:S(2)}) collective-permute-start(bf16[16,256]{1,0:T(8,128)(2,1)} %bitcast.3), channel_id=1, source_target_pairs={{32,64},{64,32},{96,128},{128,96},{160,192},{192,160},{224,256},{2... | collective-permute-start | bytes 24584 | tf_op jit(solution)/shard_map/ppermute | solution.py:275
  2.2 10.7 %collective-permute-start = (bf16[16,256]{1,0:T(8,128)(2,1)}, bf16[16,256]{1,0:T(8,128)(2,1)S(1)}, u32[]{:S(2)}, u32[]{:S(2)}) collective-permute-start(bf16[16,256]{1,0:T(8,128)(2,1)} %bitcast.4), channel_id=1, source_target_pairs={{0,32},{32,0},{64,96},{96,64},{128,160},{160,128},{192,224},{224,1... | collective-permute-start | bytes 24584 | tf_op jit(solution)/shard_map/ppermute | solution.py:274
  12.9 0.0 collective-permute-done.1.two_ref
  12.9 1.0 %collective-permute-done.one_ref = bf16[16,256]{1,0:T(8,128)(2,1)S(1)} collective-permute-done((bf16[16,256]{1,0:T(8,128)(2,1)}, bf16[16,256]{1,0:T(8,128)(2,1)S(1)}, u32[]{:S(2)}, u32[]{:S(2)}) %collective-permute-start) | collective-permute-done | bytes 8224 | tf_op jit(solution)/shard_map/ppermute | solution.py:274
  13.9 0.8 %pack.1 = bf16[32,56,128]{2,1,0:T(8,128)(2,1)S(1)} custom-call(bf16[16,256]{1,0:T(8,128)(2,1)} %bitcast.5, bf16[16,256]{1,0:T(8,128)(2,1)S(1)} %collective-permute-done.one_ref, bf16[16,256]{1,0:T(8,128)(2,1)S(1)} %collective-permute-done.1.two_ref, bf16[16,128]{1,0:T(8,128)(2,1)} %proj_ref.1), custom_call_target="tpu_custom_call" | custom-call | tf_op jit(solution)/shard_map/pack/pallas_call | solution.py:276
  14.7 27.7 %all_to_all.5.got_ref = bf16[32,56,128]{2,1,0:T(8,128)(2,1)S(1)} all-to-all(bf16[32,56,128]{2,1,0:T(8,128)(2,1)S(1)} %pack.1), channel_id=1, replica_groups=mesh['row'=16,'col'=32] {'col'}, dimensions={0} | all-to-all | bytes 917504 | tf_op jit(solution)/shard_map/all_to_all | solution.py:281
  42.4 0.3 features.1
  42.7 0.0 copy-start
  42.7 0.6 %copy-done = bf16[272,128]{1,0:T(8,128)(2,1)} copy-done((bf16[272,128]{1,0:T(8,128)(2,1)}, bf16[272,128]{1,0:T(8,128)(2,1)S(1)}, u32[]{:S(2)}) %copy-start) | copy-done | bytes 69656
  43.3 1.9 %collective-permute-start.2 = (bf16[144,128]{1,0:T(8,128)(2,1)S(1)}, bf16[144,128]{1,0:T(8,128)(2,1)S(1)}, u32[]{:S(2)}, u32[]{:S(2)}) collective-permute-start(bf16[144,128]{1,0:T(8,128)(2,1)S(1)} %get-tuple-element.14), channel_id=1, source_target_pairs={{0,160},{1,417},{2,385},{3,320},{4,128},{5,481},{6,449},{7,416},{8... | collective-permute-start | bytes 110600 | tf_op jit(solution)/shard_map/ppermute | solution.py:290
  45.2 1.3 %prepare.1 = (bf16[1152,256]{1,0:T(8,128)(2,1)S(1)}, f32[1,128]{1,0:T(1,128)S(1)}, f32[304,128]{1,0:T(8,128)S(1)}, f32[304,128]{1,0:T(8,128)S(1)}) custom-call(bf16[9,64,64]{2,1,0:T(8,128)(2,1)} %kernel_ref.1, f32[1,64]{1,0:T(1,128)} %bitcast.6, f32[1,64]{1,0:T(1,128)} %bitcast.7, bf16[272,128]{1,0:T(8,128)(2,1)} %copy-done), custom_call_target="tpu_custom_call" | custom-call | tf_op jit(solution)/shard_map/prepare/pallas_call | solution.py:188
  46.5 6.5 %collective-permute-done.2.refs_2_ = bf16[144,128]{1,0:T(8,128)(2,1)S(1)} collective-permute-done((bf16[144,128]{1,0:T(8,128)(2,1)S(1)}, bf16[144,128]{1,0:T(8,128)(2,1)S(1)}, u32[]{:S(2)}, u32[]{:S(2)}) %collective-permute-start.2) | collective-permute-done | bytes 36896 | tf_op jit(solution)/shard_map/ppermute | solution.py:290
  53.1 9.0 %pair_map.1 = bf16[256,64,128]{2,1,0:T(8,128)(2,1)} custom-call(f32[304,128]{1,0:T(8,128)S(1)} %get-tuple-element.12.refs_0_, f32[304,128]{1,0:T(8,128)S(1)} %get-tuple-element.13.refs_1_, bf16[144,128]{1,0:T(8,128)(2,1)S(1)} %collective-permute-done.2.refs_2_, bf16[1152,256]{1,0:T(8,128)(2,1)S(1)} %get-tuple-element.15.refs_3_, ...), custom_call_target="tpu_custom_call" | custom-call | tf_op jit(solution)/shard_map/pair_map/pallas_call | solution.py:200
Async XLA Ops:
  0.0 12.9 %collective-permute-start.1 = (bf16[16,256]{1,0:T(8,128)(2,1)}, bf16[16,256]{1,0:T(8,128)(2,1)S(1)}, u32[]{:S(2)}, u32[]{:S(2)}) collective-permute-start(bf16[16,256]{1,0:T(8,128)(2,1)} %bitcast.3), channel_id=1, source_target_pairs={{32,64},{64,32},{96,128},{128,96},{160,192},{192,160},{224,256},{2... | collective-permute-start | bytes 24584 | tf_op jit(solution)/shard_map/ppermute | solution.py:275
  2.2 11.7 %collective-permute-start = (bf16[16,256]{1,0:T(8,128)(2,1)}, bf16[16,256]{1,0:T(8,128)(2,1)S(1)}, u32[]{:S(2)}, u32[]{:S(2)}) collective-permute-start(bf16[16,256]{1,0:T(8,128)(2,1)} %bitcast.4), channel_id=1, source_target_pairs={{0,32},{32,0},{64,96},{96,64},{128,160},{160,128},{192,224},{224,1... | collective-permute-start | bytes 24584 | tf_op jit(solution)/shard_map/ppermute | solution.py:274
  42.7 0.6 %copy-start = (bf16[272,128]{1,0:T(8,128)(2,1)}, bf16[272,128]{1,0:T(8,128)(2,1)S(1)}, u32[]{:S(2)}) copy-start(bf16[272,128]{1,0:T(8,128)(2,1)S(1)} %get-tuple-element.11.feat_ref) | copy-start | bytes 208900
  43.3 9.7 %collective-permute-start.2 = (bf16[144,128]{1,0:T(8,128)(2,1)S(1)}, bf16[144,128]{1,0:T(8,128)(2,1)S(1)}, u32[]{:S(2)}, u32[]{:S(2)}) collective-permute-start(bf16[144,128]{1,0:T(8,128)(2,1)S(1)} %get-tuple-element.14), channel_id=1, source_target_pairs={{0,160},{1,417},{2,385},{3,320},{4,128},{5,481},{6,449},{7,416},{8... | collective-permute-start | bytes 110600 | tf_op jit(solution)/shard_map/ppermute | solution.py:290

commit v5 on v4

--- a/solution.py
+++ b/solution.py
@@ -12,7 +12,7 @@
 STEP_ROWS = GROUP * DIL
 LANES = 128
 TAPS_IN = GROUP + 2
-RING = 4
+RING = 8
 PIECE = 8
 OUT_ORDER = (1, 2, 3, 0)
 VMEM_BYTES = 48 << 20

time: 62.3 us -> 62.1 us (level)
  no operation moved by 1% of the time
where the time goes in v5:
time: 62.1 us; the launch traced here: 61.8 us
  blocking collectives  27.7 us (45%)
  starting transfers between devices  14.8 us (24%)
  Pallas kernels  11.1 us (18%)
  waiting for transfers between devices  7.53 us (12%)
  local copies, waits for them, and re-layouts  0.63 us (1%)
    all_to_all x1, blocking collectives, per_device(): got = lax.all_to_all(send, 'col', 0, 0, tiled=True)  27.7 us
    ppermute x1, starting transfers between devices, per_device(): one = lax.ppermute(own, 'row', [(r, r ^ 1) for r in range(n_row)])  10.7 us
    pallas_call x1, Pallas kernels, local_map(): pl.pallas_call(lambda *refs: map_kernel(*refs, rows=rows), grid=(rows //...  8.73 us
    ppermute x1, waiting for transfers between devices, per_device(): window = lax.ppermute(window, ('row', 'col'), window_routes(n_row, n_col))  6.53 us
    ppermute x1, starting transfers between devices, per_device(): lax.ppermute(own, 'row', [(r, (r + 1 ^ 1) - 1) for r in range(1, n_row -...  2.16 us
    ppermute x1, starting transfers between devices, per_device(): window = lax.ppermute(window, ('row', 'col'), window_routes(n_row, n_col))  1.91 us
    pallas_call x1, Pallas kernels, local_map(): pl.pallas_call(prepare_kernel, out_shape=[pltpu.VMEM((depth, GROUP * CH),...  1.3 us
  transfers between devices with their start and end apart: 3, of which 2 were waited for; matrix products, arithmetic and copies ran while one was open for 0% of the time, Pallas kernels for 2%

profile of v5, /device:TPU:6, one launch (start us, length us, event | category | flops | bytes accessed | tf_op | source)
XLA Modules:
  0.0 61.8 jit_solution(1057170042662385699)
XLA Ops:
  0.0 2.2 %collective-permute-start.1 = (bf16[16,256]{1,0:T(8,128)(2,1)}, bf16[16,256]{1,0:T(8,128)(2,1)S(1)}, u32[]{:S(2)}, u32[]{:S(2)}) collective-permute-start(bf16[16,256]{1,0:T(8,128)(2,1)} %bitcast.3), channel_id=1, source_target_pairs={{32,64},{64,32},{96,128},{128,96},{160,192},{192,160},{224,256},{2... | collective-permute-start | bytes 24584 | tf_op jit(solution)/shard_map/ppermute | solution.py:275
  2.2 10.7 %collective-permute-start = (bf16[16,256]{1,0:T(8,128)(2,1)}, bf16[16,256]{1,0:T(8,128)(2,1)S(1)}, u32[]{:S(2)}, u32[]{:S(2)}) collective-permute-start(bf16[16,256]{1,0:T(8,128)(2,1)} %bitcast.4), channel_id=1, source_target_pairs={{0,32},{32,0},{64,96},{96,64},{128,160},{160,128},{192,224},{224,1... | collective-permute-start | bytes 24584 | tf_op jit(solution)/shard_map/ppermute | solution.py:274
  12.9 0.0 collective-permute-done.1.two_ref
  12.9 1.0 %collective-permute-done.one_ref = bf16[16,256]{1,0:T(8,128)(2,1)S(1)} collective-permute-done((bf16[16,256]{1,0:T(8,128)(2,1)}, bf16[16,256]{1,0:T(8,128)(2,1)S(1)}, u32[]{:S(2)}, u32[]{:S(2)}) %collective-permute-start) | collective-permute-done | bytes 8224 | tf_op jit(solution)/shard_map/ppermute | solution.py:274
  13.9 0.8 %pack.1 = bf16[32,56,128]{2,1,0:T(8,128)(2,1)S(1)} custom-call(bf16[16,256]{1,0:T(8,128)(2,1)} %bitcast.5, bf16[16,256]{1,0:T(8,128)(2,1)S(1)} %collective-permute-done.one_ref, bf16[16,256]{1,0:T(8,128)(2,1)S(1)} %collective-permute-done.1.two_ref, bf16[16,128]{1,0:T(8,128)(2,1)} %proj_ref.1), custom_call_target="tpu_custom_call" | custom-call | tf_op jit(solution)/shard_map/pack/pallas_call | solution.py:276
  14.7 27.7 %all_to_all.5.got_ref = bf16[32,56,128]{2,1,0:T(8,128)(2,1)S(1)} all-to-all(bf16[32,56,128]{2,1,0:T(8,128)(2,1)S(1)} %pack.1), channel_id=1, replica_groups=mesh['row'=16,'col'=32] {'col'}, dimensions={0} | all-to-all | bytes 917504 | tf_op jit(solution)/shard_map/all_to_all | solution.py:281
  42.4 0.3 features.1
  42.7 0.0 copy-start
  42.7 0.6 %copy-done = bf16[272,128]{1,0:T(8,128)(2,1)} copy-done((bf16[272,128]{1,0:T(8,128)(2,1)}, bf16[272,128]{1,0:T(8,128)(2,1)S(1)}, u32[]{:S(2)}) %copy-start) | copy-done | bytes 69656
  43.3 1.9 %collective-permute-start.2 = (bf16[144,128]{1,0:T(8,128)(2,1)S(1)}, bf16[144,128]{1,0:T(8,128)(2,1)S(1)}, u32[]{:S(2)}, u32[]{:S(2)}) collective-permute-start(bf16[144,128]{1,0:T(8,128)(2,1)S(1)} %get-tuple-element.14), channel_id=1, source_target_pairs={{0,160},{1,417},{2,385},{3,320},{4,128},{5,481},{6,449},{7,416},{8... | collective-permute-start | bytes 110600 | tf_op jit(solution)/shard_map/ppermute | solution.py:290
  45.2 1.3 %prepare.1 = (bf16[1152,256]{1,0:T(8,128)(2,1)S(1)}, f32[1,128]{1,0:T(1,128)S(1)}, f32[304,128]{1,0:T(8,128)S(1)}, f32[304,128]{1,0:T(8,128)S(1)}) custom-call(bf16[9,64,64]{2,1,0:T(8,128)(2,1)} %kernel_ref.1, f32[1,64]{1,0:T(1,128)} %bitcast.6, f32[1,64]{1,0:T(1,128)} %bitcast.7, bf16[272,128]{1,0:T(8,128)(2,1)} %copy-done), custom_call_target="tpu_custom_call" | custom-call | tf_op jit(solution)/shard_map/prepare/pallas_call | solution.py:188
  46.5 6.5 %collective-permute-done.2.refs_2_ = bf16[144,128]{1,0:T(8,128)(2,1)S(1)} collective-permute-done((bf16[144,128]{1,0:T(8,128)(2,1)S(1)}, bf16[144,128]{1,0:T(8,128)(2,1)S(1)}, u32[]{:S(2)}, u32[]{:S(2)}) %collective-permute-start.2) | collective-permute-done | bytes 36896 | tf_op jit(solution)/shard_map/ppermute | solution.py:290
  53.1 8.7 %pair_map.1 = bf16[256,64,128]{2,1,0:T(8,128)(2,1)} custom-call(f32[304,128]{1,0:T(8,128)S(1)} %get-tuple-element.12.refs_0_, f32[304,128]{1,0:T(8,128)S(1)} %get-tuple-element.13.refs_1_, bf16[144,128]{1,0:T(8,128)(2,1)S(1)} %collective-permute-done.2.refs_2_, bf16[1152,256]{1,0:T(8,128)(2,1)S(1)} %get-tuple-element.15.refs_3_, ...), custom_call_target="tpu_custom_call" | custom-call | tf_op jit(solution)/shard_map/pair_map/pallas_call | solution.py:200
Async XLA Ops:
  0.0 12.9 %collective-permute-start.1 = (bf16[16,256]{1,0:T(8,128)(2,1)}, bf16[16,256]{1,0:T(8,128)(2,1)S(1)}, u32[]{:S(2)}, u32[]{:S(2)}) collective-permute-start(bf16[16,256]{1,0:T(8,128)(2,1)} %bitcast.3), channel_id=1, source_target_pairs={{32,64},{64,32},{96,128},{128,96},{160,192},{192,160},{224,256},{2... | collective-permute-start | bytes 24584 | tf_op jit(solution)/shard_map/ppermute | solution.py:275
  2.2 11.7 %collective-permute-start = (bf16[16,256]{1,0:T(8,128)(2,1)}, bf16[16,256]{1,0:T(8,128)(2,1)S(1)}, u32[]{:S(2)}, u32[]{:S(2)}) collective-permute-start(bf16[16,256]{1,0:T(8,128)(2,1)} %bitcast.4), channel_id=1, source_target_pairs={{0,32},{32,0},{64,96},{96,64},{128,160},{160,128},{192,224},{224,1... | collective-permute-start | bytes 24584 | tf_op jit(solution)/shard_map/ppermute | solution.py:274
  42.7 0.6 %copy-start = (bf16[272,128]{1,0:T(8,128)(2,1)}, bf16[272,128]{1,0:T(8,128)(2,1)S(1)}, u32[]{:S(2)}) copy-start(bf16[272,128]{1,0:T(8,128)(2,1)S(1)} %get-tuple-element.11.feat_ref) | copy-start | bytes 208900
  43.3 9.7 %collective-permute-start.2 = (bf16[144,128]{1,0:T(8,128)(2,1)S(1)}, bf16[144,128]{1,0:T(8,128)(2,1)S(1)}, u32[]{:S(2)}, u32[]{:S(2)}) collective-permute-start(bf16[144,128]{1,0:T(8,128)(2,1)S(1)} %get-tuple-element.14), channel_id=1, source_target_pairs={{0,160},{1,417},{2,385},{3,320},{4,128},{5,481},{6,449},{7,416},{8... | collective-permute-start | bytes 110600 | tf_op jit(solution)/shard_map/ppermute | solution.py:290
